TPU v7x, 256 devices: a whole 4x4x8 slice. The times are simulated.
256 devices in a mesh: dp: 32 (over z, y_hi, core), fsdp: 8 (over y_lo, x).
Axes of the slice: x: 4, y: 4 (y_hi: 2, y_lo: 2; y = y_hi * 2 + y_lo), z: 8, core: 2. Of those that a mesh axis runs over, the one named last changes fastest.
Arguments:
- hidden: bfloat16 [131072, 1152], P(('dp', 'fsdp')), may hold values from -6 to 6
- text_ids: int32 [8192, 16], P(('dp', 'fsdp')), may hold values from 0 to 31999, as said below
- ln_gain: float32 [1152], replicated, may hold values from 0.5 to 1.5
- ln_bias: float32 [1152], replicated, may hold values from -2 to 2
- fc1_weight: bfloat16 [1152, 4304], P(None, 'fsdp'), may hold values from -0.1875 to 0.1875
- fc1_bias: float32 [4304], replicated, may hold values from -3 to 3
- fc2_weight: bfloat16 [4304, 1152], P('fsdp'), may hold values from -0.09375 to 0.09375
- fc2_bias: float32 [1152], replicated, may hold values from -3 to 3
- final_gain: float32 [1152], replicated, may hold values from 0.5 to 1.5
- final_bias: float32 [1152], replicated, may hold values from -0.2 to 0.2
- head_weight: bfloat16 [1152, 1152], replicated, may hold values from -0.1875 to 0.1875
- head_bias: float32 [1152], replicated, may hold values from -0.3 to 0.3
- image_emb: bfloat16 [8192, 1152], P(('dp', 'fsdp')), may hold values from -6 to 6
- teacher_logits: bfloat16 [8192, 12, 256], P('dp', None, 'fsdp'), may hold values from -12 to 12
- logit_scale: float32 [1], replicated, may hold values from 4 to 16
- logit_bias: float32 [1], replicated, may hold values from -3 to 0
Outputs:
- image_grad: float32 [8192, 1152], P(('dp', 'fsdp'))
Inputs may be any that keep to these rules, and one draw needn't show every extreme that they name: `text_ids`: 0 marks padding after a text's end; every text has at least one token and the tokens of a text come first.
All inputs are finite; a program needn't handle non-finite values.
Results may differ from a plain program's by a relative error of at most 0.0018.
Values may be sent and summed in bfloat16 or wider, within the bound.
No kernel may reach another device: no remote copies, remote signals or barrier semaphores. Data moves between devices by JAX's collectives and lax.ppermute only.
A program may use at most 128 MiB of HBM per device.

v0:
```python
import jax
import jax.numpy as jnp
from jax import lax
from jax.sharding import PartitionSpec as P


def from_everyone(array, axis):
    copies = jnp.broadcast_to(array, (lax.axis_size(axis), *array.shape))
    return lax.all_to_all(copies, axis, split_axis=0, concat_axis=0, tiled=True)


def joined_along(parts, dim):
    parts = jnp.moveaxis(parts, 0, dim)
    dims = parts.shape
    return parts.reshape(*dims[:dim], dims[dim] * dims[dim + 1], *dims[dim + 2 :])


def gather_directly(array, axis, dim):
    parts = from_everyone(array, axis)
    return joined_along(parts, dim)


def from_behind(array, axis, by):
    count = lax.axis_size(axis)
    return lax.ppermute(array, axis, [(i, (i + by) % count) for i in range(count)])


def layer_norm(values, gain, shift):
    centre = jnp.mean(values, axis=-1, keepdims=True)
    spread = jnp.mean((values - centre) ** 2, axis=-1, keepdims=True)
    return (values - centre) * lax.rsqrt(spread + 1e-06) * gain + shift


def on_device(
    hidden,
    text_ids,
    ln_gain,
    ln_bias,
    fc1_weight,
    fc1_bias,
    fc2_weight,
    fc2_bias,
    final_gain,
    final_bias,
    head_weight,
    head_bias,
    image_emb,
    teacher_logits,
    logit_scale,
    logit_bias,
):
    width = hidden.shape[1]
    texts_here, seq_len = text_ids.shape
    window = teacher_logits.shape[1]
    flat = hidden.astype(jnp.float32)
    normed = layer_norm(flat, ln_gain, ln_bias).astype(jnp.bfloat16)
    pre = (
        jnp.dot(
            normed,
            lax.all_gather(fc1_weight, "fsdp", axis=1, tiled=True),
            preferred_element_type=jnp.float32,
        )
        + fc1_bias
    )
    act = jax.nn.gelu(pre, approximate=True).astype(jnp.bfloat16)
    mixed = jnp.dot(
        act,
        lax.all_gather(fc2_weight, "fsdp", axis=0, tiled=True),
        preferred_element_type=jnp.float32,
    )
    out = flat + mixed + fc2_bias
    final = layer_norm(out, final_gain, final_bias).reshape(texts_here, seq_len, width)
    keep = (text_ids != 0).astype(jnp.float32)
    pooled = jnp.sum(final * keep[:, :, None], axis=1) / jnp.sum(keep, axis=1)[:, None]
    emb = (
        jnp.dot(pooled.astype(jnp.bfloat16), head_weight, preferred_element_type=jnp.float32)
        + head_bias
    )
    text_unit = (emb * lax.rsqrt(jnp.sum(emb * emb, axis=-1, keepdims=True) + 1e-06)).astype(
        jnp.bfloat16
    )
    group_units = gather_directly(text_unit, "fsdp", 0)
    images = image_emb.astype(jnp.float32)
    image_unit = (
        images * lax.rsqrt(jnp.sum(images * images, axis=-1, keepdims=True) + 1e-06)
    ).astype(jnp.bfloat16)
    scale = logit_scale[0]
    offset = logit_bias[0]

    def pair_term(units, pictures, tile):
        score = (
            scale
            * lax.dot_general(
                units, pictures, (((1,), (1,)), ((), ())), preferred_element_type=jnp.float32
            )
            + offset
        )
        weight = (jax.nn.sigmoid(score) - jax.nn.sigmoid(tile.astype(jnp.float32))).astype(
            jnp.bfloat16
        )
        return lax.dot_general(
            weight, units, (((0,), (0,)), ((), ())), preferred_element_type=jnp.float32
        )

    start_grad = jnp.zeros(image_unit.shape, jnp.float32)

    def turn_images(step, carry):
        pictures, total = carry
        tile = lax.dynamic_index_in_dim(teacher_logits, step, 1, keepdims=False)
        total = total + pair_term(group_units, pictures, tile)
        pictures, total = (
            from_behind(pictures.astype(jnp.float32), "dp", -1).astype(pictures.dtype),
            from_behind(total, "dp", -1),
        )
        return (pictures, total)

    pictures, total = lax.fori_loop(0, window - 1, turn_images, (image_unit, start_grad))
    total = total + pair_term(group_units, pictures, teacher_logits[:, window - 1, :])
    total = from_behind(total, "dp", window - 1)
    return scale * total


def solution(mesh):
    placed = (
        P(("dp", "fsdp"), None),
        P(("dp", "fsdp"), None),
        P(),
        P(),
        P(None, "fsdp"),
        P(),
        P("fsdp", None),
        P(),
        P(),
        P(),
        P(),
        P(),
        P(("dp", "fsdp"), None),
        P("dp", None, "fsdp"),
        P(),
        P(),
    )
    return jax.shard_map(
        on_device, mesh=mesh, in_specs=placed, out_specs=P(("dp", "fsdp"), None), check_vma=False
    )
```

profile of v0, /device:TPU:1, one launch (start us, length us, event | category | flops | bytes accessed | tf_op | source)
XLA Modules:
  0.0 442.1 jit_solution(9942454543745646307)
XLA Ops:
  8.3 1.5 convert_reduce_fusion
  9.8 1.7 fusion.31
  11.5 111.0 %all-gather.5.cloned.1.call-done = bf16[8,538,1152]{2,1,0:T(8,128)(2,1)} async-done(((bf16[1,538,1152]{2,1,0:T(8,128)(2,1)}), bf16[8,538,1152]{2,1,0:T(8,128)(2,1)}) %all-gather.5.cloned.1.call-update) | async-done | bytes 9916432 | tf_op jit(solution)/shard_map/all_gather | solution.py:60
  122.5 11.8 %reshape.68 = bf16[4304,1152]{1,0:T(8,128)(2,1)} reshape(bf16[8,538,1152]{2,1,0:T(8,128)(2,1)} %all-gather.5.cloned.1.call-done) | data formatting | bytes 19832832
  134.4 98.5 %all-gather.7.cloned.1.call-done = bf16[8,538,1152]{2,1,0:T(8,128)(2,1)} async-done(((bf16[1,538,1152]{2,1,0:T(8,128)(2,1)}), bf16[8,538,1152]{2,1,0:T(8,128)(2,1)}) %all-gather.7.cloned.1.call-update) | async-done | bytes 9916432 | tf_op jit(solution)/shard_map/all_gather | solution.py:68
  232.9 11.9 %reshape.70 = bf16[4304,1152]{1,0:T(8,128)(2,1)} reshape(bf16[8,538,1152]{2,1,0:T(8,128)(2,1)} %all-gather.7.cloned.1.call-done) | data formatting | bytes 19832832
  244.8 23.1 %fusion.72 = (f32[512]{0:T(512)S(1)}, f32[512,1152]{1,0:T(8,128)}) fusion(f32[1152]{0:T(1024)S(1)} %copy-done.8, bf16[4304,1152]{1,0:T(8,128)(2,1)} %reshape.70, bf16[4304,1152]{1,0:T(8,128)(2,1)} %reshape.68, f32[4304]{0:T(1024)S(1)} %copy-done.7, bf16[512,1152]{1,0:T(8,128)(2,1)} %param.18, f32[1152]{0:T(1024)S(1)} %copy-done.9, f32[1152]{0:T(1024)S(1)} %copy-done.10, ...), kind=kOutput, calls=%fused_computation.91 | convolution fusion | flops 10182344704 | bytes 23408960 | tf_op jit(solution)/shard_map/dot_general | solution.py:66
  268.0 2.2 multiply_reduce_fusion.1
  272.9 3.5 all-to-all-start
  277.8 9.5 %all-to-all-done = bf16[8,32,1152]{2,1,0:T(8,128)(2,1)S(1)} async-done(((bf16[8,32,1152]{2,1,0:T(8,128)(2,1)}), bf16[8,32,1152]{2,1,0:T(8,128)(2,1)S(1)}, u32[]{:S(2)}, u32[]{:S(2)}) %all-to-all-start) | async-done | bytes 589856 | tf_op jit(solution)/shard_map/all_to_all | solution.py:9
  287.3 134.7 %while.15 = (s32[]{:T(128)}, bf16[32,1152]{1,0:T(8,128)(2,1)S(1)}, f32[32,1152]{1,0:T(8,128)S(1)}, f32[]{:T(128)}, bf16[256,1152]{1,0:T(8,128)(2,1)S(1)}, /*inde...) while((s32[]{:T(128)}, bf16[32,1152]{1,0:T(8,128)(2,1)S(1)}, f32[32,1152]{1,0:T(8,128)S(1)}, f32[]{:T(128)}, ...), condition=%wide.region_9.10_spmd, body=%wide.region_8.9_spmd.sunk | while | flops 37875712 | bytes 2598565 | solution.py:117
  287.4 3.3 convolution_add_fusion.4
  291.4 4.8 %collective-permute-start = (bf16[32,1152]{1,0:T(8,128)(2,1)S(1)}, bf16[32,1152]{1,0:T(8,128)(2,1)S(1)}, u32[]{:S(2)}, u32[]{:S(2)}) collective-permute-start(bf16[32,1152]{1,0:T(8,128)(2,1)S(1)} %copy.24), channel_id=1, source_target_pairs={{0,248},{8,0},{16,8},{24,16},{32,24},{40,32},{48,40},{56,48},{64,5... | collective-permute-start | bytes 221192 | tf_op jit(solution)/shard_map/while/body/eval_jaxpr/ppermute | solution.py:25
  296.2 1.5 collective-permute-done
  297.7 3.3 convolution_add_fusion.4
  301.0 2.2 collective-permute-start.1
  303.2 5.5 %collective-permute-start = (bf16[32,1152]{1,0:T(8,128)(2,1)S(1)}, bf16[32,1152]{1,0:T(8,128)(2,1)S(1)}, u32[]{:S(2)}, u32[]{:S(2)}) collective-permute-start(bf16[32,1152]{1,0:T(8,128)(2,1)S(1)} %copy.24), channel_id=1, source_target_pairs={{0,248},{8,0},{16,8},{24,16},{32,24},{40,32},{48,40},{56,48},{64,5... | collective-permute-start | bytes 221192 | tf_op jit(solution)/shard_map/while/body/eval_jaxpr/ppermute | solution.py:25
  308.7 0.9 collective-permute-done
  309.7 3.3 convolution_add_fusion.4
  312.9 2.7 collective-permute-start.1
  315.7 5.5 %collective-permute-start = (bf16[32,1152]{1,0:T(8,128)(2,1)S(1)}, bf16[32,1152]{1,0:T(8,128)(2,1)S(1)}, u32[]{:S(2)}, u32[]{:S(2)}) collective-permute-start(bf16[32,1152]{1,0:T(8,128)(2,1)S(1)} %copy.24), channel_id=1, source_target_pairs={{0,248},{8,0},{16,8},{24,16},{32,24},{40,32},{48,40},{56,48},{64,5... | collective-permute-start | bytes 221192 | tf_op jit(solution)/shard_map/while/body/eval_jaxpr/ppermute | solution.py:25
  322.1 3.3 convolution_add_fusion.4
  325.4 2.7 collective-permute-start.1
  328.2 5.5 %collective-permute-start = (bf16[32,1152]{1,0:T(8,128)(2,1)S(1)}, bf16[32,1152]{1,0:T(8,128)(2,1)S(1)}, u32[]{:S(2)}, u32[]{:S(2)}) collective-permute-start(bf16[32,1152]{1,0:T(8,128)(2,1)S(1)} %copy.24), channel_id=1, source_target_pairs={{0,248},{8,0},{16,8},{24,16},{32,24},{40,32},{48,40},{56,48},{64,5... | collective-permute-start | bytes 221192 | tf_op jit(solution)/shard_map/while/body/eval_jaxpr/ppermute | solution.py:25
  334.6 3.3 convolution_add_fusion.4
  337.9 2.7 collective-permute-start.1
  340.7 5.5 %collective-permute-start = (bf16[32,1152]{1,0:T(8,128)(2,1)S(1)}, bf16[32,1152]{1,0:T(8,128)(2,1)S(1)}, u32[]{:S(2)}, u32[]{:S(2)}) collective-permute-start(bf16[32,1152]{1,0:T(8,128)(2,1)S(1)} %copy.24), channel_id=1, source_target_pairs={{0,248},{8,0},{16,8},{24,16},{32,24},{40,32},{48,40},{56,48},{64,5... | collective-permute-start | bytes 221192 | tf_op jit(solution)/shard_map/while/body/eval_jaxpr/ppermute | solution.py:25
  346.2 0.9 collective-permute-done
  347.1 3.3 convolution_add_fusion.4
  350.4 2.7 collective-permute-start.1
  353.1 5.5 %collective-permute-start = (bf16[32,1152]{1,0:T(8,128)(2,1)S(1)}, bf16[32,1152]{1,0:T(8,128)(2,1)S(1)}, u32[]{:S(2)}, u32[]{:S(2)}) collective-permute-start(bf16[32,1152]{1,0:T(8,128)(2,1)S(1)} %copy.24), channel_id=1, source_target_pairs={{0,248},{8,0},{16,8},{24,16},{32,24},{40,32},{48,40},{56,48},{64,5... | collective-permute-start | bytes 221192 | tf_op jit(solution)/shard_map/while/body/eval_jaxpr/ppermute | solution.py:25
  359.6 3.3 convolution_add_fusion.4
  362.9 2.7 collective-permute-start.1
  365.6 5.5 %collective-permute-start = (bf16[32,1152]{1,0:T(8,128)(2,1)S(1)}, bf16[32,1152]{1,0:T(8,128)(2,1)S(1)}, u32[]{:S(2)}, u32[]{:S(2)}) collective-permute-start(bf16[32,1152]{1,0:T(8,128)(2,1)S(1)} %copy.24), channel_id=1, source_target_pairs={{0,248},{8,0},{16,8},{24,16},{32,24},{40,32},{48,40},{56,48},{64,5... | collective-permute-start | bytes 221192 | tf_op jit(solution)/shard_map/while/body/eval_jaxpr/ppermute | solution.py:25
  372.1 3.3 convolution_add_fusion.4
  375.4 2.7 collective-permute-start.1
  378.1 5.5 %collective-permute-start = (bf16[32,1152]{1,0:T(8,128)(2,1)S(1)}, bf16[32,1152]{1,0:T(8,128)(2,1)S(1)}, u32[]{:S(2)}, u32[]{:S(2)}) collective-permute-start(bf16[32,1152]{1,0:T(8,128)(2,1)S(1)} %copy.24), channel_id=1, source_target_pairs={{0,248},{8,0},{16,8},{24,16},{32,24},{40,32},{48,40},{56,48},{64,5... | collective-permute-start | bytes 221192 | tf_op jit(solution)/shard_map/while/body/eval_jaxpr/ppermute | solution.py:25
  384.6 3.3 convolution_add_fusion.4
  387.9 2.7 collective-permute-start.1
  390.6 5.5 %collective-permute-start = (bf16[32,1152]{1,0:T(8,128)(2,1)S(1)}, bf16[32,1152]{1,0:T(8,128)(2,1)S(1)}, u32[]{:S(2)}, u32[]{:S(2)}) collective-permute-start(bf16[32,1152]{1,0:T(8,128)(2,1)S(1)} %copy.24), channel_id=1, source_target_pairs={{0,248},{8,0},{16,8},{24,16},{32,24},{40,32},{48,40},{56,48},{64,5... | collective-permute-start | bytes 221192 | tf_op jit(solution)/shard_map/while/body/eval_jaxpr/ppermute | solution.py:25
  397.1 3.3 convolution_add_fusion.4
  400.3 2.7 collective-permute-start.1
  403.1 5.5 %collective-permute-start = (bf16[32,1152]{1,0:T(8,128)(2,1)S(1)}, bf16[32,1152]{1,0:T(8,128)(2,1)S(1)}, u32[]{:S(2)}, u32[]{:S(2)}) collective-permute-start(bf16[32,1152]{1,0:T(8,128)(2,1)S(1)} %copy.24), channel_id=1, source_target_pairs={{0,248},{8,0},{16,8},{24,16},{32,24},{40,32},{48,40},{56,48},{64,5... | collective-permute-start | bytes 221192 | tf_op jit(solution)/shard_map/while/body/eval_jaxpr/ppermute | solution.py:25
  409.5 3.3 convolution_add_fusion.4
  412.8 2.7 collective-permute-start.1
  415.6 5.5 %collective-permute-start = (bf16[32,1152]{1,0:T(8,128)(2,1)S(1)}, bf16[32,1152]{1,0:T(8,128)(2,1)S(1)}, u32[]{:S(2)}, u32[]{:S(2)}) collective-permute-start(bf16[32,1152]{1,0:T(8,128)(2,1)S(1)} %copy.24), channel_id=1, source_target_pairs={{0,248},{8,0},{16,8},{24,16},{32,24},{40,32},{48,40},{56,48},{64,5... | collective-permute-start | bytes 221192 | tf_op jit(solution)/shard_map/while/body/eval_jaxpr/ppermute | solution.py:25
  422.0 2.0 convolution_add_fusion.1
  424.0 10.6 %collective-permute-done.2 = f32[32,1152]{1,0:T(8,128)S(1)} collective-permute-done((f32[32,1152]{1,0:T(8,128)}, f32[32,1152]{1,0:T(8,128)S(1)}, u32[]{:S(2)}, u32[]{:S(2)}) %collective-permute-start.2) | collective-permute-done | bytes 147488 | tf_op jit(solution)/shard_map/ppermute | solution.py:25
  (75 shorter events, 13.4 us)
Async XLA Ops:
  6.5 264.6 %copy-start = (bf16[1152,1152]{1,0:T(8,128)(2,1)S(1)}, bf16[1152,1152]{1,0:T(8,128)(2,1)}, u32[]{:S(2)}) copy-start(bf16[1152,1152]{1,0:T(8,128)(2,1)} %param.28) | copy-start | bytes 7962628
  6.5 1.5 copy-start.3
  6.5 1.6 copy-start.2
  6.5 116.0 %all-gather.5.cloned.1.call-start = ((), (), s32[]{:S(2)}) async-start(), calls=%async_computation.1 | async-start | bytes 11280384 | tf_op jit(solution)/shard_map/all_gather | solution.py:60
  7.3 225.6 %all-gather.7.cloned.1.call-start = ((), (), s32[]{:S(2)}) async-start(), calls=%async_computation.2 | async-start | bytes 11280384 | tf_op jit(solution)/shard_map/all_gather | solution.py:68
  134.3 110.5 %copy-start.7 = (f32[4304]{0:T(1024)S(1)}, f32[4304]{0:T(1024)}, u32[]{:S(2)}) copy-start(f32[4304]{0:T(1024)} %param.23) | copy-start | bytes 51652
  134.4 110.5 %copy-start.8 = (f32[1152]{0:T(1024)S(1)}, f32[1152]{0:T(1024)}, u32[]{:S(2)}) copy-start(f32[1152]{0:T(1024)} %param.25) | copy-start | bytes 13828
  134.4 110.5 %copy-start.9 = (f32[1152]{0:T(1024)S(1)}, f32[1152]{0:T(1024)}, u32[]{:S(2)}) copy-start(f32[1152]{0:T(1024)} %param.21) | copy-start | bytes 13828
  134.4 110.5 %copy-start.10 = (f32[1152]{0:T(1024)S(1)}, f32[1152]{0:T(1024)}, u32[]{:S(2)}) copy-start(f32[1152]{0:T(1024)} %param.20) | copy-start | bytes 13828
  244.8 25.3 %copy-start.5 = (f32[1152]{0:T(1024)S(1)}, f32[1152]{0:T(1024)}, u32[]{:S(2)}) copy-start(f32[1152]{0:T(1024)} %param.26) | copy-start | bytes 13828
  267.9 2.4 copy-start.1
  267.9 2.4 copy-start.4
  267.9 3.2 copy-start.6
  272.9 14.4 %all-to-all-start = ((bf16[8,32,1152]{2,1,0:T(8,128)(2,1)}), bf16[8,32,1152]{2,1,0:T(8,128)(2,1)S(1)}, u32[]{:S(2)}, u32[]{:S(2)}) async-start(bf16[8,32,1152]{2,1,0:T(8,128)(2,1)} %broadcast_in_dim.5), calls=%async_computation | async-start | bytes 1179648 | tf_op jit(solution)/shard_map/all_to_all | solution.py:9
  290.7 7.1 %collective-permute-start.1 = (f32[32,1152]{1,0:T(8,128)}, f32[32,1152]{1,0:T(8,128)S(1)}, u32[]{:S(2)}, u32[]{:S(2)}) collective-permute-start(f32[32,1152]{1,0:T(8,128)} %convolution_add_fusion.4), channel_id=1, source_target_pairs={{0,248},{8,0},{16,8},{24,16},{32,24},{40,32},{48,40},{56,48},{64,5... | collective-permute-start | bytes 442376 | tf_op jit(solution)/shard_map/while/body/eval_jaxpr/ppermute | solution.py:25
  291.4 6.3 %collective-permute-start = (bf16[32,1152]{1,0:T(8,128)(2,1)S(1)}, bf16[32,1152]{1,0:T(8,128)(2,1)S(1)}, u32[]{:S(2)}, u32[]{:S(2)}) collective-permute-start(bf16[32,1152]{1,0:T(8,128)(2,1)S(1)} %copy.24), channel_id=1, source_target_pairs={{0,248},{8,0},{16,8},{24,16},{32,24},{40,32},{48,40},{56,48},{64,5... | collective-permute-start | bytes 221192 | tf_op jit(solution)/shard_map/while/body/eval_jaxpr/ppermute | solution.py:25
  301.0 8.6 %collective-permute-start.1 = (f32[32,1152]{1,0:T(8,128)}, f32[32,1152]{1,0:T(8,128)S(1)}, u32[]{:S(2)}, u32[]{:S(2)}) collective-permute-start(f32[32,1152]{1,0:T(8,128)} %convolution_add_fusion.4), channel_id=1, source_target_pairs={{0,248},{8,0},{16,8},{24,16},{32,24},{40,32},{48,40},{56,48},{64,5... | collective-permute-start | bytes 442376 | tf_op jit(solution)/shard_map/while/body/eval_jaxpr/ppermute | solution.py:25
  303.2 6.4 %collective-permute-start = (bf16[32,1152]{1,0:T(8,128)(2,1)S(1)}, bf16[32,1152]{1,0:T(8,128)(2,1)S(1)}, u32[]{:S(2)}, u32[]{:S(2)}) collective-permute-start(bf16[32,1152]{1,0:T(8,128)(2,1)S(1)} %copy.24), channel_id=1, source_target_pairs={{0,248},{8,0},{16,8},{24,16},{32,24},{40,32},{48,40},{56,48},{64,5... | collective-permute-start | bytes 221192 | tf_op jit(solution)/shard_map/while/body/eval_jaxpr/ppermute | solution.py:25
  312.9 9.2 %collective-permute-start.1 = (f32[32,1152]{1,0:T(8,128)}, f32[32,1152]{1,0:T(8,128)S(1)}, u32[]{:S(2)}, u32[]{:S(2)}) collective-permute-start(f32[32,1152]{1,0:T(8,128)} %convolution_add_fusion.4), channel_id=1, source_target_pairs={{0,248},{8,0},{16,8},{24,16},{32,24},{40,32},{48,40},{56,48},{64,5... | collective-permute-start | bytes 442376 | tf_op jit(solution)/shard_map/while/body/eval_jaxpr/ppermute | solution.py:25
  315.7 6.4 %collective-permute-start = (bf16[32,1152]{1,0:T(8,128)(2,1)S(1)}, bf16[32,1152]{1,0:T(8,128)(2,1)S(1)}, u32[]{:S(2)}, u32[]{:S(2)}) collective-permute-start(bf16[32,1152]{1,0:T(8,128)(2,1)S(1)} %copy.24), channel_id=1, source_target_pairs={{0,248},{8,0},{16,8},{24,16},{32,24},{40,32},{48,40},{56,48},{64,5... | collective-permute-start | bytes 221192 | tf_op jit(solution)/shard_map/while/body/eval_jaxpr/ppermute | solution.py:25
  325.4 9.2 %collective-permute-start.1 = (f32[32,1152]{1,0:T(8,128)}, f32[32,1152]{1,0:T(8,128)S(1)}, u32[]{:S(2)}, u32[]{:S(2)}) collective-permute-start(f32[32,1152]{1,0:T(8,128)} %convolution_add_fusion.4), channel_id=1, source_target_pairs={{0,248},{8,0},{16,8},{24,16},{32,24},{40,32},{48,40},{56,48},{64,5... | collective-permute-start | bytes 442376 | tf_op jit(solution)/shard_map/while/body/eval_jaxpr/ppermute | solution.py:25
  328.2 6.4 %collective-permute-start = (bf16[32,1152]{1,0:T(8,128)(2,1)S(1)}, bf16[32,1152]{1,0:T(8,128)(2,1)S(1)}, u32[]{:S(2)}, u32[]{:S(2)}) collective-permute-start(bf16[32,1152]{1,0:T(8,128)(2,1)S(1)} %copy.24), channel_id=1, source_target_pairs={{0,248},{8,0},{16,8},{24,16},{32,24},{40,32},{48,40},{56,48},{64,5... | collective-permute-start | bytes 221192 | tf_op jit(solution)/shard_map/while/body/eval_jaxpr/ppermute | solution.py:25
  337.9 9.2 %collective-permute-start.1 = (f32[32,1152]{1,0:T(8,128)}, f32[32,1152]{1,0:T(8,128)S(1)}, u32[]{:S(2)}, u32[]{:S(2)}) collective-permute-start(f32[32,1152]{1,0:T(8,128)} %convolution_add_fusion.4), channel_id=1, source_target_pairs={{0,248},{8,0},{16,8},{24,16},{32,24},{40,32},{48,40},{56,48},{64,5... | collective-permute-start | bytes 442376 | tf_op jit(solution)/shard_map/while/body/eval_jaxpr/ppermute | solution.py:25
  340.7 6.4 %collective-permute-start = (bf16[32,1152]{1,0:T(8,128)(2,1)S(1)}, bf16[32,1152]{1,0:T(8,128)(2,1)S(1)}, u32[]{:S(2)}, u32[]{:S(2)}) collective-permute-start(bf16[32,1152]{1,0:T(8,128)(2,1)S(1)} %copy.24), channel_id=1, source_target_pairs={{0,248},{8,0},{16,8},{24,16},{32,24},{40,32},{48,40},{56,48},{64,5... | collective-permute-start | bytes 221192 | tf_op jit(solution)/shard_map/while/body/eval_jaxpr/ppermute | solution.py:25
  350.4 9.2 %collective-permute-start.1 = (f32[32,1152]{1,0:T(8,128)}, f32[32,1152]{1,0:T(8,128)S(1)}, u32[]{:S(2)}, u32[]{:S(2)}) collective-permute-start(f32[32,1152]{1,0:T(8,128)} %convolution_add_fusion.4), channel_id=1, source_target_pairs={{0,248},{8,0},{16,8},{24,16},{32,24},{40,32},{48,40},{56,48},{64,5... | collective-permute-start | bytes 442376 | tf_op jit(solution)/shard_map/while/body/eval_jaxpr/ppermute | solution.py:25
  353.1 6.4 %collective-permute-start = (bf16[32,1152]{1,0:T(8,128)(2,1)S(1)}, bf16[32,1152]{1,0:T(8,128)(2,1)S(1)}, u32[]{:S(2)}, u32[]{:S(2)}) collective-permute-start(bf16[32,1152]{1,0:T(8,128)(2,1)S(1)} %copy.24), channel_id=1, source_target_pairs={{0,248},{8,0},{16,8},{24,16},{32,24},{40,32},{48,40},{56,48},{64,5... | collective-permute-start | bytes 221192 | tf_op jit(solution)/shard_map/while/body/eval_jaxpr/ppermute | solution.py:25
  362.9 9.2 %collective-permute-start.1 = (f32[32,1152]{1,0:T(8,128)}, f32[32,1152]{1,0:T(8,128)S(1)}, u32[]{:S(2)}, u32[]{:S(2)}) collective-permute-start(f32[32,1152]{1,0:T(8,128)} %convolution_add_fusion.4), channel_id=1, source_target_pairs={{0,248},{8,0},{16,8},{24,16},{32,24},{40,32},{48,40},{56,48},{64,5... | collective-permute-start | bytes 442376 | tf_op jit(solution)/shard_map/while/body/eval_jaxpr/ppermute | solution.py:25
  365.6 6.4 %collective-permute-start = (bf16[32,1152]{1,0:T(8,128)(2,1)S(1)}, bf16[32,1152]{1,0:T(8,128)(2,1)S(1)}, u32[]{:S(2)}, u32[]{:S(2)}) collective-permute-start(bf16[32,1152]{1,0:T(8,128)(2,1)S(1)} %copy.24), channel_id=1, source_target_pairs={{0,248},{8,0},{16,8},{24,16},{32,24},{40,32},{48,40},{56,48},{64,5... | collective-permute-start | bytes 221192 | tf_op jit(solution)/shard_map/while/body/eval_jaxpr/ppermute | solution.py:25
  375.4 9.2 %collective-permute-start.1 = (f32[32,1152]{1,0:T(8,128)}, f32[32,1152]{1,0:T(8,128)S(1)}, u32[]{:S(2)}, u32[]{:S(2)}) collective-permute-start(f32[32,1152]{1,0:T(8,128)} %convolution_add_fusion.4), channel_id=1, source_target_pairs={{0,248},{8,0},{16,8},{24,16},{32,24},{40,32},{48,40},{56,48},{64,5... | collective-permute-start | bytes 442376 | tf_op jit(solution)/shard_map/while/body/eval_jaxpr/ppermute | solution.py:25
  378.1 6.4 %collective-permute-start = (bf16[32,1152]{1,0:T(8,128)(2,1)S(1)}, bf16[32,1152]{1,0:T(8,128)(2,1)S(1)}, u32[]{:S(2)}, u32[]{:S(2)}) collective-permute-start(bf16[32,1152]{1,0:T(8,128)(2,1)S(1)} %copy.24), channel_id=1, source_target_pairs={{0,248},{8,0},{16,8},{24,16},{32,24},{40,32},{48,40},{56,48},{64,5... | collective-permute-start | bytes 221192 | tf_op jit(solution)/shard_map/while/body/eval_jaxpr/ppermute | solution.py:25
  387.9 9.2 %collective-permute-start.1 = (f32[32,1152]{1,0:T(8,128)}, f32[32,1152]{1,0:T(8,128)S(1)}, u32[]{:S(2)}, u32[]{:S(2)}) collective-permute-start(f32[32,1152]{1,0:T(8,128)} %convolution_add_fusion.4), channel_id=1, source_target_pairs={{0,248},{8,0},{16,8},{24,16},{32,24},{40,32},{48,40},{56,48},{64,5... | collective-permute-start | bytes 442376 | tf_op jit(solution)/shard_map/while/body/eval_jaxpr/ppermute | solution.py:25
  390.6 6.4 %collective-permute-start = (bf16[32,1152]{1,0:T(8,128)(2,1)S(1)}, bf16[32,1152]{1,0:T(8,128)(2,1)S(1)}, u32[]{:S(2)}, u32[]{:S(2)}) collective-permute-start(bf16[32,1152]{1,0:T(8,128)(2,1)S(1)} %copy.24), channel_id=1, source_target_pairs={{0,248},{8,0},{16,8},{24,16},{32,24},{40,32},{48,40},{56,48},{64,5... | collective-permute-start | bytes 221192 | tf_op jit(solution)/shard_map/while/body/eval_jaxpr/ppermute | solution.py:25
  400.3 9.2 %collective-permute-start.1 = (f32[32,1152]{1,0:T(8,128)}, f32[32,1152]{1,0:T(8,128)S(1)}, u32[]{:S(2)}, u32[]{:S(2)}) collective-permute-start(f32[32,1152]{1,0:T(8,128)} %convolution_add_fusion.4), channel_id=1, source_target_pairs={{0,248},{8,0},{16,8},{24,16},{32,24},{40,32},{48,40},{56,48},{64,5... | collective-permute-start | bytes 442376 | tf_op jit(solution)/shard_map/while/body/eval_jaxpr/ppermute | solution.py:25
  403.1 6.4 %collective-permute-start = (bf16[32,1152]{1,0:T(8,128)(2,1)S(1)}, bf16[32,1152]{1,0:T(8,128)(2,1)S(1)}, u32[]{:S(2)}, u32[]{:S(2)}) collective-permute-start(bf16[32,1152]{1,0:T(8,128)(2,1)S(1)} %copy.24), channel_id=1, source_target_pairs={{0,248},{8,0},{16,8},{24,16},{32,24},{40,32},{48,40},{56,48},{64,5... | collective-permute-start | bytes 221192 | tf_op jit(solution)/shard_map/while/body/eval_jaxpr/ppermute | solution.py:25
  412.8 9.2 %collective-permute-start.1 = (f32[32,1152]{1,0:T(8,128)}, f32[32,1152]{1,0:T(8,128)S(1)}, u32[]{:S(2)}, u32[]{:S(2)}) collective-permute-start(f32[32,1152]{1,0:T(8,128)} %convolution_add_fusion.4), channel_id=1, source_target_pairs={{0,248},{8,0},{16,8},{24,16},{32,24},{40,32},{48,40},{56,48},{64,5... | collective-permute-start | bytes 442376 | tf_op jit(solution)/shard_map/while/body/eval_jaxpr/ppermute | solution.py:25
  415.6 6.4 %collective-permute-start = (bf16[32,1152]{1,0:T(8,128)(2,1)S(1)}, bf16[32,1152]{1,0:T(8,128)(2,1)S(1)}, u32[]{:S(2)}, u32[]{:S(2)}) collective-permute-start(bf16[32,1152]{1,0:T(8,128)(2,1)S(1)} %copy.24), channel_id=1, source_target_pairs={{0,248},{8,0},{16,8},{24,16},{32,24},{40,32},{48,40},{56,48},{64,5... | collective-permute-start | bytes 221192 | tf_op jit(solution)/shard_map/while/body/eval_jaxpr/ppermute | solution.py:25
  424.0 10.6 %collective-permute-start.2 = (f32[32,1152]{1,0:T(8,128)}, f32[32,1152]{1,0:T(8,128)S(1)}, u32[]{:S(2)}, u32[]{:S(2)}) collective-permute-start(f32[32,1152]{1,0:T(8,128)} %convolution_add_fusion.1), channel_id=1, source_target_pairs={{0,88},{8,96},{16,104},{24,112},{32,120},{40,128},{48,136},{56,144... | collective-permute-start | bytes 442376 | tf_op jit(solution)/shard_map/ppermute | solution.py:25
Sparse Core Ops, SparseCore 0:
  9.1 113.3 all-gather.4
  124.3 108.5 all-gather.6
where the time goes:
time: 444 us; the launch traced here: 442 us
  waiting for transfers between devices  242 us (55%)
  starting transfers between devices  91.3 us (21%)
  matrix products  62 us (14%)
  local copies, waits for them, and re-layouts  25 us (6%)
  between operations  14.8 us (3%)
  other arithmetic  7.29 us (2%)
    all_gather x1, waiting for transfers between devices, on_device(): lax.all_gather(fc1_weight, 'fsdp', axis=1, tiled=True)  111 us
    all_gather x1, waiting for transfers between devices, on_device(): lax.all_gather(fc2_weight, 'fsdp', axis=0, tiled=True)  98.5 us
    ppermute x23, starting transfers between devices, from_behind(): lax.ppermute(array, axis, [(i, (i + by) % count) for i in range(count)])  87.7 us
    dot_general x12, matrix products, pair_term(): lax.dot_general(weight, units, (((0,), (0,)), ((), ())), preferred_elemen...  38.2 us
    unnamed x24, local copies, waits for them, and re-layouts  23.9 us
    dot_general x1, matrix products, on_device(): jnp.dot(act, lax.all_gather(fc2_weight, 'fsdp', axis=0, tiled=True), pref...  23.1 us
    ppermute x23, waiting for transfers between devices, from_behind(): lax.ppermute(array, axis, [(i, (i + by) % count) for i in range(count)])  21.2 us
    all_to_all x1, waiting for transfers between devices, from_everyone(): return lax.all_to_all(copies, axis, split_axis=0, concat_axis=0, tiled=True)  9.5 us
  transfers between devices with their start and end apart: 26, of which 15 were waited for; matrix products, arithmetic and copies ran while one was open for 3% of the time, Pallas kernels for 0%

commit v1 on v0

--- a/solution.py
+++ b/solution.py
@@ -2,6 +2,11 @@
 import jax.numpy as jnp
 from jax import lax
 from jax.sharding import PartitionSpec as P
+
+
+def direct_records(here_x):
+    latest = jnp.concatenate(lax.all_gather(here_x, "fsdp"), 1)
+    return latest
 
 
 def from_everyone(array, axis):
@@ -54,14 +59,7 @@
     window = teacher_logits.shape[1]
     flat = hidden.astype(jnp.float32)
     normed = layer_norm(flat, ln_gain, ln_bias).astype(jnp.bfloat16)
-    pre = (
-        jnp.dot(
-            normed,
-            lax.all_gather(fc1_weight, "fsdp", axis=1, tiled=True),
-            preferred_element_type=jnp.float32,
-        )
-        + fc1_bias
-    )
+    pre = jnp.dot(normed, direct_records(fc1_weight), preferred_element_type=jnp.float32) + fc1_bias
     act = jax.nn.gelu(pre, approximate=True).astype(jnp.bfloat16)
     mixed = jnp.dot(
         act,

time: 444 us -> 444 us (level)
  waiting for transfers between devices: 242 us -> 214 us
  local copies, waits for them, and re-layouts: 25 us -> 52.6 us
    all_gather x1, waiting for transfers between devices: 98.5 us -> 70.8 us  [on_device(): lax.all_gather(fc2_weight, 'fsdp', axis=0, tiled=True)]
    all_gather x0 -> x2, local copies, waits for them, and re-layouts: none -> 17.7 us  [direct_records(): latest = jnp.concatenate(lax.all_gather(here_x, 'fsdp'), 1)]
    reshape x0 -> x1, local copies, waits for them, and re-layouts: none -> 12 us  [direct_records(): latest = jnp.concatenate(lax.all_gather(here_x, 'fsdp'), 1)]
  transfers between devices with their start and end apart: 26 -> 26, of which waited for: 15 -> 15; matrix products, arithmetic and copies ran while one was open for 3% -> 10% of each run, Pallas kernels for 0% -> 0%
where the time goes in v1:
time: 444 us; the launch traced here: 442 us
  waiting for transfers between devices  214 us (48%)
  starting transfers between devices  91.3 us (21%)
  matrix products  62 us (14%)
  local copies, waits for them, and re-layouts  52.6 us (12%)
  between operations  14.8 us (3%)
  other arithmetic  7.29 us (2%)
    all_gather x1, waiting for transfers between devices, direct_records(): latest = jnp.concatenate(lax.all_gather(here_x, 'fsdp'), 1)  111 us
    ppermute x23, starting transfers between devices, from_behind(): lax.ppermute(array, axis, [(i, (i + by) % count) for i in range(count)])  87.7 us
    all_gather x1, waiting for transfers between devices, on_device(): lax.all_gather(fc2_weight, 'fsdp', axis=0, tiled=True)  70.8 us
    dot_general x12, matrix products, pair_term(): lax.dot_general(weight, units, (((0,), (0,)), ((), ())), preferred_elemen...  38.2 us
    dot_general x1, matrix products, on_device(): jnp.dot(act, lax.all_gather(fc2_weight, 'fsdp', axis=0, tiled=True), pref...  23.1 us
    unnamed x24, local copies, waits for them, and re-layouts  21.9 us
    ppermute x23, waiting for transfers between devices, from_behind(): lax.ppermute(array, axis, [(i, (i + by) % count) for i in range(count)])  21.2 us
    all_gather x2, local copies, waits for them, and re-layouts, direct_records(): latest = jnp.concatenate(lax.all_gather(here_x, 'fsdp'), 1)  17.7 us
  transfers between devices with their start and end apart: 26, of which 15 were waited for; matrix products, arithmetic and copies ran while one was open for 10% of the time, Pallas kernels for 0%

profile of v1, /device:TPU:1, one launch (start us, length us, event | category | flops | bytes accessed | tf_op | source)
XLA Modules:
  0.0 442.0 jit_solution(16784996015665665445)
XLA Ops:
  8.3 1.5 convert_reduce_fusion
  9.8 1.7 fusion.31
  11.5 111.0 %all-gather.5.cloned.1.call-done = bf16[9216,538]{0,1:T(8,128)(2,1)} async-done(((bf16[1152,538]{0,1:T(8,128)(2,1)}), bf16[9216,538]{0,1:T(8,128)(2,1)}) %all-gather.5.cloned.1.call-update) | async-done | bytes 9916432 | tf_op jit(solution)/shard_map/all_gather | solution.py:8
  122.5 9.9 %copy.22 = bf16[68,8,8,1152]{3,2,1,0:T(8,128)(2,1)} copy(bf16[68,8,8,1152]{3,1,2,0:T(8,128)(2,1)} %bitcast.50) | data formatting | bytes 20054016
  132.5 8.7 %slice_bitcast_fusion = bf16[8,1152,538]{1,0,2:T(8,128)(2,1)} fusion(bf16[544,8,1152]{2,1,0:T(8,128)(2,1)} %bitcast.49), kind=kLoop, calls=%fused_computation.24 | loop fusion | bytes 19832832 | tf_op jit(solution)/shard_map/all_gather | solution.py:8
  141.2 8.9 %copy.24 = bf16[8,1152,538]{1,2,0:T(8,128)(2,1)} copy(bf16[8,1152,538]{1,0,2:T(8,128)(2,1)} %slice_bitcast_fusion) | data formatting | bytes 19832832 | tf_op jit(solution)/shard_map/all_gather | solution.py:8
  150.1 12.0 %reshape.68 = bf16[1152,4304]{0,1:T(8,128)(2,1)} reshape(bf16[1152,8,538]{0,2,1:T(8,128)(2,1)} %bitcast.48) | data formatting | bytes 19832832 | tf_op jit(solution)/shard_map/reshape | solution.py:8
  162.2 70.8 %all-gather.7.cloned.1.call-done = bf16[8,538,1152]{2,1,0:T(8,128)(2,1)} async-done(((bf16[1,538,1152]{2,1,0:T(8,128)(2,1)}), bf16[8,538,1152]{2,1,0:T(8,128)(2,1)}) %all-gather.7.cloned.1.call-update) | async-done | bytes 9916432 | tf_op jit(solution)/shard_map/all_gather | solution.py:66
  232.9 11.8 %reshape.77 = bf16[4304,1152]{1,0:T(8,128)(2,1)} reshape(bf16[8,538,1152]{2,1,0:T(8,128)(2,1)} %all-gather.7.cloned.1.call-done) | data formatting | bytes 19832832
  244.8 23.1 %fusion.72 = (f32[512]{0:T(512)S(1)}, f32[512,1152]{1,0:T(8,128)}) fusion(f32[1152]{0:T(1024)S(1)} %copy-done.8, bf16[4304,1152]{1,0:T(8,128)(2,1)} %reshape.77, bf16[1152,4304]{0,1:T(8,128)(2,1)} %reshape.68, f32[4304]{0:T(1024)S(1)} %copy-done.7, bf16[512,1152]{1,0:T(8,128)(2,1)} %param.18, f32[1152]{0:T(1024)S(1)} %copy-done.9, f32[1152]{0:T(1024)S(1)} %copy-done.10, ...), kind=kOutput, calls=%fused_computation.93 | convolution fusion | flops 10182344704 | bytes 23408960 | tf_op jit(solution)/shard_map/dot_general | solution.py:64
  267.9 2.2 multiply_reduce_fusion.1
  272.8 3.5 all-to-all-start
  277.8 9.5 %all-to-all-done = bf16[8,32,1152]{2,1,0:T(8,128)(2,1)S(1)} async-done(((bf16[8,32,1152]{2,1,0:T(8,128)(2,1)}), bf16[8,32,1152]{2,1,0:T(8,128)(2,1)S(1)}, u32[]{:S(2)}, u32[]{:S(2)}) %all-to-all-start) | async-done | bytes 589856 | tf_op jit(solution)/shard_map/all_to_all | solution.py:14
  287.3 134.7 %while.15 = (s32[]{:T(128)}, bf16[32,1152]{1,0:T(8,128)(2,1)S(1)}, f32[32,1152]{1,0:T(8,128)S(1)}, f32[]{:T(128)}, bf16[256,1152]{1,0:T(8,128)(2,1)S(1)}, /*inde...) while((s32[]{:T(128)}, bf16[32,1152]{1,0:T(8,128)(2,1)S(1)}, f32[32,1152]{1,0:T(8,128)S(1)}, f32[]{:T(128)}, ...), condition=%wide.region_9.10_spmd, body=%wide.region_8.9_spmd.sunk | while | flops 37875712 | bytes 2598565 | solution.py:115
  287.3 3.3 convolution_add_fusion.4
  291.4 4.8 %collective-permute-start = (bf16[32,1152]{1,0:T(8,128)(2,1)S(1)}, bf16[32,1152]{1,0:T(8,128)(2,1)S(1)}, u32[]{:S(2)}, u32[]{:S(2)}) collective-permute-start(bf16[32,1152]{1,0:T(8,128)(2,1)S(1)} %copy.29), channel_id=1, source_target_pairs={{0,248},{8,0},{16,8},{24,16},{32,24},{40,32},{48,40},{56,48},{64,5... | collective-permute-start | bytes 221192 | tf_op jit(solution)/shard_map/while/body/eval_jaxpr/ppermute | solution.py:30
  297.7 3.3 convolution_add_fusion.4
  301.0 2.2 collective-permute-start.1
  303.1 5.5 %collective-permute-start = (bf16[32,1152]{1,0:T(8,128)(2,1)S(1)}, bf16[32,1152]{1,0:T(8,128)(2,1)S(1)}, u32[]{:S(2)}, u32[]{:S(2)}) collective-permute-start(bf16[32,1152]{1,0:T(8,128)(2,1)S(1)} %copy.29), channel_id=1, source_target_pairs={{0,248},{8,0},{16,8},{24,16},{32,24},{40,32},{48,40},{56,48},{64,5... | collective-permute-start | bytes 221192 | tf_op jit(solution)/shard_map/while/body/eval_jaxpr/ppermute | solution.py:30
  309.6 3.3 convolution_add_fusion.4
  312.9 2.7 collective-permute-start.1
  315.6 5.5 %collective-permute-start = (bf16[32,1152]{1,0:T(8,128)(2,1)S(1)}, bf16[32,1152]{1,0:T(8,128)(2,1)S(1)}, u32[]{:S(2)}, u32[]{:S(2)}) collective-permute-start(bf16[32,1152]{1,0:T(8,128)(2,1)S(1)} %copy.29), channel_id=1, source_target_pairs={{0,248},{8,0},{16,8},{24,16},{32,24},{40,32},{48,40},{56,48},{64,5... | collective-permute-start | bytes 221192 | tf_op jit(solution)/shard_map/while/body/eval_jaxpr/ppermute | solution.py:30
  322.1 3.3 convolution_add_fusion.4
  325.4 2.7 collective-permute-start.1
  328.1 5.5 %collective-permute-start = (bf16[32,1152]{1,0:T(8,128)(2,1)S(1)}, bf16[32,1152]{1,0:T(8,128)(2,1)S(1)}, u32[]{:S(2)}, u32[]{:S(2)}) collective-permute-start(bf16[32,1152]{1,0:T(8,128)(2,1)S(1)} %copy.29), channel_id=1, source_target_pairs={{0,248},{8,0},{16,8},{24,16},{32,24},{40,32},{48,40},{56,48},{64,5... | collective-permute-start | bytes 221192 | tf_op jit(solution)/shard_map/while/body/eval_jaxpr/ppermute | solution.py:30
  334.6 3.3 convolution_add_fusion.4
  337.8 2.7 collective-permute-start.1
  340.6 5.5 %collective-permute-start = (bf16[32,1152]{1,0:T(8,128)(2,1)S(1)}, bf16[32,1152]{1,0:T(8,128)(2,1)S(1)}, u32[]{:S(2)}, u32[]{:S(2)}) collective-permute-start(bf16[32,1152]{1,0:T(8,128)(2,1)S(1)} %copy.29), channel_id=1, source_target_pairs={{0,248},{8,0},{16,8},{24,16},{32,24},{40,32},{48,40},{56,48},{64,5... | collective-permute-start | bytes 221192 | tf_op jit(solution)/shard_map/while/body/eval_jaxpr/ppermute | solution.py:30
  347.0 3.3 convolution_add_fusion.4
  350.3 2.7 collective-permute-start.1
  353.1 5.5 %collective-permute-start = (bf16[32,1152]{1,0:T(8,128)(2,1)S(1)}, bf16[32,1152]{1,0:T(8,128)(2,1)S(1)}, u32[]{:S(2)}, u32[]{:S(2)}) collective-permute-start(bf16[32,1152]{1,0:T(8,128)(2,1)S(1)} %copy.29), channel_id=1, source_target_pairs={{0,248},{8,0},{16,8},{24,16},{32,24},{40,32},{48,40},{56,48},{64,5... | collective-permute-start | bytes 221192 | tf_op jit(solution)/shard_map/while/body/eval_jaxpr/ppermute | solution.py:30
  359.5 3.3 convolution_add_fusion.4
  362.8 2.7 collective-permute-start.1
  365.6 5.5 %collective-permute-start = (bf16[32,1152]{1,0:T(8,128)(2,1)S(1)}, bf16[32,1152]{1,0:T(8,128)(2,1)S(1)}, u32[]{:S(2)}, u32[]{:S(2)}) collective-permute-start(bf16[32,1152]{1,0:T(8,128)(2,1)S(1)} %copy.29), channel_id=1, source_target_pairs={{0,248},{8,0},{16,8},{24,16},{32,24},{40,32},{48,40},{56,48},{64,5... | collective-permute-start | bytes 221192 | tf_op jit(solution)/shard_map/while/body/eval_jaxpr/ppermute | solution.py:30
  372.0 3.3 convolution_add_fusion.4
  375.3 2.7 collective-permute-start.1
  378.0 5.5 %collective-permute-start = (bf16[32,1152]{1,0:T(8,128)(2,1)S(1)}, bf16[32,1152]{1,0:T(8,128)(2,1)S(1)}, u32[]{:S(2)}, u32[]{:S(2)}) collective-permute-start(bf16[32,1152]{1,0:T(8,128)(2,1)S(1)} %copy.29), channel_id=1, source_target_pairs={{0,248},{8,0},{16,8},{24,16},{32,24},{40,32},{48,40},{56,48},{64,5... | collective-permute-start | bytes 221192 | tf_op jit(solution)/shard_map/while/body/eval_jaxpr/ppermute | solution.py:30
  384.5 3.3 convolution_add_fusion.4
  387.8 2.7 collective-permute-start.1
  390.5 5.5 %collective-permute-start = (bf16[32,1152]{1,0:T(8,128)(2,1)S(1)}, bf16[32,1152]{1,0:T(8,128)(2,1)S(1)}, u32[]{:S(2)}, u32[]{:S(2)}) collective-permute-start(bf16[32,1152]{1,0:T(8,128)(2,1)S(1)} %copy.29), channel_id=1, source_target_pairs={{0,248},{8,0},{16,8},{24,16},{32,24},{40,32},{48,40},{56,48},{64,5... | collective-permute-start | bytes 221192 | tf_op jit(solution)/shard_map/while/body/eval_jaxpr/ppermute | solution.py:30
  397.0 3.3 convolution_add_fusion.4
  400.3 2.7 collective-permute-start.1
  403.0 5.5 %collective-permute-start = (bf16[32,1152]{1,0:T(8,128)(2,1)S(1)}, bf16[32,1152]{1,0:T(8,128)(2,1)S(1)}, u32[]{:S(2)}, u32[]{:S(2)}) collective-permute-start(bf16[32,1152]{1,0:T(8,128)(2,1)S(1)} %copy.29), channel_id=1, source_target_pairs={{0,248},{8,0},{16,8},{24,16},{32,24},{40,32},{48,40},{56,48},{64,5... | collective-permute-start | bytes 221192 | tf_op jit(solution)/shard_map/while/body/eval_jaxpr/ppermute | solution.py:30
  409.5 3.3 convolution_add_fusion.4
  412.8 2.7 collective-permute-start.1
  415.5 5.5 %collective-permute-start = (bf16[32,1152]{1,0:T(8,128)(2,1)S(1)}, bf16[32,1152]{1,0:T(8,128)(2,1)S(1)}, u32[]{:S(2)}, u32[]{:S(2)}) collective-permute-start(bf16[32,1152]{1,0:T(8,128)(2,1)S(1)} %copy.29), channel_id=1, source_target_pairs={{0,248},{8,0},{16,8},{24,16},{32,24},{40,32},{48,40},{56,48},{64,5... | collective-permute-start | bytes 221192 | tf_op jit(solution)/shard_map/while/body/eval_jaxpr/ppermute | solution.py:30
  421.9 2.0 convolution_add_fusion.1
  423.9 10.6 %collective-permute-done.2 = f32[32,1152]{1,0:T(8,128)S(1)} collective-permute-done((f32[32,1152]{1,0:T(8,128)}, f32[32,1152]{1,0:T(8,128)S(1)}, u32[]{:S(2)}, u32[]{:S(2)}) %collective-permute-start.2) | collective-permute-done | bytes 147488 | tf_op jit(solution)/shard_map/ppermute | solution.py:30
  (78 shorter events, 16.7 us)
Async XLA Ops:
  6.5 264.6 %copy-start = (bf16[1152,1152]{1,0:T(8,128)(2,1)S(1)}, bf16[1152,1152]{1,0:T(8,128)(2,1)}, u32[]{:S(2)}) copy-start(bf16[1152,1152]{1,0:T(8,128)(2,1)} %param.28) | copy-start | bytes 7962628
  6.5 1.5 copy-start.3
  6.5 1.6 copy-start.2
  6.5 116.0 %all-gather.5.cloned.1.call-start = ((), (), s32[]{:S(2)}) async-start(), calls=%async_computation.1 | async-start | bytes 11280384 | tf_op jit(solution)/shard_map/all_gather | solution.py:8
  7.3 225.6 %all-gather.7.cloned.1.call-start = ((), (), s32[]{:S(2)}) async-start(), calls=%async_computation.2 | async-start | bytes 11280384 | tf_op jit(solution)/shard_map/all_gather | solution.py:66
  162.1 82.6 %copy-start.7 = (f32[4304]{0:T(1024)S(1)}, f32[4304]{0:T(1024)}, u32[]{:S(2)}) copy-start(f32[4304]{0:T(1024)} %param.23) | copy-start | bytes 51652
  162.1 82.6 %copy-start.8 = (f32[1152]{0:T(1024)S(1)}, f32[1152]{0:T(1024)}, u32[]{:S(2)}) copy-start(f32[1152]{0:T(1024)} %param.25) | copy-start | bytes 13828
  162.1 82.6 %copy-start.9 = (f32[1152]{0:T(1024)S(1)}, f32[1152]{0:T(1024)}, u32[]{:S(2)}) copy-start(f32[1152]{0:T(1024)} %param.21) | copy-start | bytes 13828
  162.1 82.6 %copy-start.10 = (f32[1152]{0:T(1024)S(1)}, f32[1152]{0:T(1024)}, u32[]{:S(2)}) copy-start(f32[1152]{0:T(1024)} %param.20) | copy-start | bytes 13828
  244.7 25.3 %copy-start.5 = (f32[1152]{0:T(1024)S(1)}, f32[1152]{0:T(1024)}, u32[]{:S(2)}) copy-start(f32[1152]{0:T(1024)} %param.26) | copy-start | bytes 13828
  267.8 2.4 copy-start.1
  267.8 2.4 copy-start.4
  267.9 3.2 copy-start.6
  272.8 14.4 %all-to-all-start = ((bf16[8,32,1152]{2,1,0:T(8,128)(2,1)}), bf16[8,32,1152]{2,1,0:T(8,128)(2,1)S(1)}, u32[]{:S(2)}, u32[]{:S(2)}) async-start(bf16[8,32,1152]{2,1,0:T(8,128)(2,1)} %broadcast_in_dim.5), calls=%async_computation | async-start | bytes 1179648 | tf_op jit(solution)/shard_map/all_to_all | solution.py:14
  290.6 7.1 %collective-permute-start.1 = (f32[32,1152]{1,0:T(8,128)}, f32[32,1152]{1,0:T(8,128)S(1)}, u32[]{:S(2)}, u32[]{:S(2)}) collective-permute-start(f32[32,1152]{1,0:T(8,128)} %convolution_add_fusion.4), channel_id=1, source_target_pairs={{0,248},{8,0},{16,8},{24,16},{32,24},{40,32},{48,40},{56,48},{64,5... | collective-permute-start | bytes 442376 | tf_op jit(solution)/shard_map/while/body/eval_jaxpr/ppermute | solution.py:30
  291.4 6.3 %collective-permute-start = (bf16[32,1152]{1,0:T(8,128)(2,1)S(1)}, bf16[32,1152]{1,0:T(8,128)(2,1)S(1)}, u32[]{:S(2)}, u32[]{:S(2)}) collective-permute-start(bf16[32,1152]{1,0:T(8,128)(2,1)S(1)} %copy.29), channel_id=1, source_target_pairs={{0,248},{8,0},{16,8},{24,16},{32,24},{40,32},{48,40},{56,48},{64,5... | collective-permute-start | bytes 221192 | tf_op jit(solution)/shard_map/while/body/eval_jaxpr/ppermute | solution.py:30
  301.0 8.6 %collective-permute-start.1 = (f32[32,1152]{1,0:T(8,128)}, f32[32,1152]{1,0:T(8,128)S(1)}, u32[]{:S(2)}, u32[]{:S(2)}) collective-permute-start(f32[32,1152]{1,0:T(8,128)} %convolution_add_fusion.4), channel_id=1, source_target_pairs={{0,248},{8,0},{16,8},{24,16},{32,24},{40,32},{48,40},{56,48},{64,5... | collective-permute-start | bytes 442376 | tf_op jit(solution)/shard_map/while/body/eval_jaxpr/ppermute | solution.py:30
  303.1 6.4 %collective-permute-start = (bf16[32,1152]{1,0:T(8,128)(2,1)S(1)}, bf16[32,1152]{1,0:T(8,128)(2,1)S(1)}, u32[]{:S(2)}, u32[]{:S(2)}) collective-permute-start(bf16[32,1152]{1,0:T(8,128)(2,1)S(1)} %copy.29), channel_id=1, source_target_pairs={{0,248},{8,0},{16,8},{24,16},{32,24},{40,32},{48,40},{56,48},{64,5... | collective-permute-start | bytes 221192 | tf_op jit(solution)/shard_map/while/body/eval_jaxpr/ppermute | solution.py:30
  312.9 9.2 %collective-permute-start.1 = (f32[32,1152]{1,0:T(8,128)}, f32[32,1152]{1,0:T(8,128)S(1)}, u32[]{:S(2)}, u32[]{:S(2)}) collective-permute-start(f32[32,1152]{1,0:T(8,128)} %convolution_add_fusion.4), channel_id=1, source_target_pairs={{0,248},{8,0},{16,8},{24,16},{32,24},{40,32},{48,40},{56,48},{64,5... | collective-permute-start | bytes 442376 | tf_op jit(solution)/shard_map/while/body/eval_jaxpr/ppermute | solution.py:30
  315.6 6.4 %collective-permute-start = (bf16[32,1152]{1,0:T(8,128)(2,1)S(1)}, bf16[32,1152]{1,0:T(8,128)(2,1)S(1)}, u32[]{:S(2)}, u32[]{:S(2)}) collective-permute-start(bf16[32,1152]{1,0:T(8,128)(2,1)S(1)} %copy.29), channel_id=1, source_target_pairs={{0,248},{8,0},{16,8},{24,16},{32,24},{40,32},{48,40},{56,48},{64,5... | collective-permute-start | bytes 221192 | tf_op jit(solution)/shard_map/while/body/eval_jaxpr/ppermute | solution.py:30
  325.4 9.2 %collective-permute-start.1 = (f32[32,1152]{1,0:T(8,128)}, f32[32,1152]{1,0:T(8,128)S(1)}, u32[]{:S(2)}, u32[]{:S(2)}) collective-permute-start(f32[32,1152]{1,0:T(8,128)} %convolution_add_fusion.4), channel_id=1, source_target_pairs={{0,248},{8,0},{16,8},{24,16},{32,24},{40,32},{48,40},{56,48},{64,5... | collective-permute-start | bytes 442376 | tf_op jit(solution)/shard_map/while/body/eval_jaxpr/ppermute | solution.py:30
  328.1 6.4 %collective-permute-start = (bf16[32,1152]{1,0:T(8,128)(2,1)S(1)}, bf16[32,1152]{1,0:T(8,128)(2,1)S(1)}, u32[]{:S(2)}, u32[]{:S(2)}) collective-permute-start(bf16[32,1152]{1,0:T(8,128)(2,1)S(1)} %copy.29), channel_id=1, source_target_pairs={{0,248},{8,0},{16,8},{24,16},{32,24},{40,32},{48,40},{56,48},{64,5... | collective-permute-start | bytes 221192 | tf_op jit(solution)/shard_map/while/body/eval_jaxpr/ppermute | solution.py:30
  337.8 9.2 %collective-permute-start.1 = (f32[32,1152]{1,0:T(8,128)}, f32[32,1152]{1,0:T(8,128)S(1)}, u32[]{:S(2)}, u32[]{:S(2)}) collective-permute-start(f32[32,1152]{1,0:T(8,128)} %convolution_add_fusion.4), channel_id=1, source_target_pairs={{0,248},{8,0},{16,8},{24,16},{32,24},{40,32},{48,40},{56,48},{64,5... | collective-permute-start | bytes 442376 | tf_op jit(solution)/shard_map/while/body/eval_jaxpr/ppermute | solution.py:30
  340.6 6.4 %collective-permute-start = (bf16[32,1152]{1,0:T(8,128)(2,1)S(1)}, bf16[32,1152]{1,0:T(8,128)(2,1)S(1)}, u32[]{:S(2)}, u32[]{:S(2)}) collective-permute-start(bf16[32,1152]{1,0:T(8,128)(2,1)S(1)} %copy.29), channel_id=1, source_target_pairs={{0,248},{8,0},{16,8},{24,16},{32,24},{40,32},{48,40},{56,48},{64,5... | collective-permute-start | bytes 221192 | tf_op jit(solution)/shard_map/while/body/eval_jaxpr/ppermute | solution.py:30
  350.3 9.2 %collective-permute-start.1 = (f32[32,1152]{1,0:T(8,128)}, f32[32,1152]{1,0:T(8,128)S(1)}, u32[]{:S(2)}, u32[]{:S(2)}) collective-permute-start(f32[32,1152]{1,0:T(8,128)} %convolution_add_fusion.4), channel_id=1, source_target_pairs={{0,248},{8,0},{16,8},{24,16},{32,24},{40,32},{48,40},{56,48},{64,5... | collective-permute-start | bytes 442376 | tf_op jit(solution)/shard_map/while/body/eval_jaxpr/ppermute | solution.py:30
  353.1 6.4 %collective-permute-start = (bf16[32,1152]{1,0:T(8,128)(2,1)S(1)}, bf16[32,1152]{1,0:T(8,128)(2,1)S(1)}, u32[]{:S(2)}, u32[]{:S(2)}) collective-permute-start(bf16[32,1152]{1,0:T(8,128)(2,1)S(1)} %copy.29), channel_id=1, source_target_pairs={{0,248},{8,0},{16,8},{24,16},{32,24},{40,32},{48,40},{56,48},{64,5... | collective-permute-start | bytes 221192 | tf_op jit(solution)/shard_map/while/body/eval_jaxpr/ppermute | solution.py:30
  362.8 9.2 %collective-permute-start.1 = (f32[32,1152]{1,0:T(8,128)}, f32[32,1152]{1,0:T(8,128)S(1)}, u32[]{:S(2)}, u32[]{:S(2)}) collective-permute-start(f32[32,1152]{1,0:T(8,128)} %convolution_add_fusion.4), channel_id=1, source_target_pairs={{0,248},{8,0},{16,8},{24,16},{32,24},{40,32},{48,40},{56,48},{64,5... | collective-permute-start | bytes 442376 | tf_op jit(solution)/shard_map/while/body/eval_jaxpr/ppermute | solution.py:30
  365.6 6.4 %collective-permute-start = (bf16[32,1152]{1,0:T(8,128)(2,1)S(1)}, bf16[32,1152]{1,0:T(8,128)(2,1)S(1)}, u32[]{:S(2)}, u32[]{:S(2)}) collective-permute-start(bf16[32,1152]{1,0:T(8,128)(2,1)S(1)} %copy.29), channel_id=1, source_target_pairs={{0,248},{8,0},{16,8},{24,16},{32,24},{40,32},{48,40},{56,48},{64,5... | collective-permute-start | bytes 221192 | tf_op jit(solution)/shard_map/while/body/eval_jaxpr/ppermute | solution.py:30
  375.3 9.2 %collective-permute-start.1 = (f32[32,1152]{1,0:T(8,128)}, f32[32,1152]{1,0:T(8,128)S(1)}, u32[]{:S(2)}, u32[]{:S(2)}) collective-permute-start(f32[32,1152]{1,0:T(8,128)} %convolution_add_fusion.4), channel_id=1, source_target_pairs={{0,248},{8,0},{16,8},{24,16},{32,24},{40,32},{48,40},{56,48},{64,5... | collective-permute-start | bytes 442376 | tf_op jit(solution)/shard_map/while/body/eval_jaxpr/ppermute | solution.py:30
  378.0 6.4 %collective-permute-start = (bf16[32,1152]{1,0:T(8,128)(2,1)S(1)}, bf16[32,1152]{1,0:T(8,128)(2,1)S(1)}, u32[]{:S(2)}, u32[]{:S(2)}) collective-permute-start(bf16[32,1152]{1,0:T(8,128)(2,1)S(1)} %copy.29), channel_id=1, source_target_pairs={{0,248},{8,0},{16,8},{24,16},{32,24},{40,32},{48,40},{56,48},{64,5... | collective-permute-start | bytes 221192 | tf_op jit(solution)/shard_map/while/body/eval_jaxpr/ppermute | solution.py:30
  387.8 9.2 %collective-permute-start.1 = (f32[32,1152]{1,0:T(8,128)}, f32[32,1152]{1,0:T(8,128)S(1)}, u32[]{:S(2)}, u32[]{:S(2)}) collective-permute-start(f32[32,1152]{1,0:T(8,128)} %convolution_add_fusion.4), channel_id=1, source_target_pairs={{0,248},{8,0},{16,8},{24,16},{32,24},{40,32},{48,40},{56,48},{64,5... | collective-permute-start | bytes 442376 | tf_op jit(solution)/shard_map/while/body/eval_jaxpr/ppermute | solution.py:30
  390.5 6.4 %collective-permute-start = (bf16[32,1152]{1,0:T(8,128)(2,1)S(1)}, bf16[32,1152]{1,0:T(8,128)(2,1)S(1)}, u32[]{:S(2)}, u32[]{:S(2)}) collective-permute-start(bf16[32,1152]{1,0:T(8,128)(2,1)S(1)} %copy.29), channel_id=1, source_target_pairs={{0,248},{8,0},{16,8},{24,16},{32,24},{40,32},{48,40},{56,48},{64,5... | collective-permute-start | bytes 221192 | tf_op jit(solution)/shard_map/while/body/eval_jaxpr/ppermute | solution.py:30
  400.3 9.2 %collective-permute-start.1 = (f32[32,1152]{1,0:T(8,128)}, f32[32,1152]{1,0:T(8,128)S(1)}, u32[]{:S(2)}, u32[]{:S(2)}) collective-permute-start(f32[32,1152]{1,0:T(8,128)} %convolution_add_fusion.4), channel_id=1, source_target_pairs={{0,248},{8,0},{16,8},{24,16},{32,24},{40,32},{48,40},{56,48},{64,5... | collective-permute-start | bytes 442376 | tf_op jit(solution)/shard_map/while/body/eval_jaxpr/ppermute | solution.py:30
  403.0 6.4 %collective-permute-start = (bf16[32,1152]{1,0:T(8,128)(2,1)S(1)}, bf16[32,1152]{1,0:T(8,128)(2,1)S(1)}, u32[]{:S(2)}, u32[]{:S(2)}) collective-permute-start(bf16[32,1152]{1,0:T(8,128)(2,1)S(1)} %copy.29), channel_id=1, source_target_pairs={{0,248},{8,0},{16,8},{24,16},{32,24},{40,32},{48,40},{56,48},{64,5... | collective-permute-start | bytes 221192 | tf_op jit(solution)/shard_map/while/body/eval_jaxpr/ppermute | solution.py:30
  412.8 9.2 %collective-permute-start.1 = (f32[32,1152]{1,0:T(8,128)}, f32[32,1152]{1,0:T(8,128)S(1)}, u32[]{:S(2)}, u32[]{:S(2)}) collective-permute-start(f32[32,1152]{1,0:T(8,128)} %convolution_add_fusion.4), channel_id=1, source_target_pairs={{0,248},{8,0},{16,8},{24,16},{32,24},{40,32},{48,40},{56,48},{64,5... | collective-permute-start | bytes 442376 | tf_op jit(solution)/shard_map/while/body/eval_jaxpr/ppermute | solution.py:30
  415.5 6.4 %collective-permute-start = (bf16[32,1152]{1,0:T(8,128)(2,1)S(1)}, bf16[32,1152]{1,0:T(8,128)(2,1)S(1)}, u32[]{:S(2)}, u32[]{:S(2)}) collective-permute-start(bf16[32,1152]{1,0:T(8,128)(2,1)S(1)} %copy.29), channel_id=1, source_target_pairs={{0,248},{8,0},{16,8},{24,16},{32,24},{40,32},{48,40},{56,48},{64,5... | collective-permute-start | bytes 221192 | tf_op jit(solution)/shard_map/while/body/eval_jaxpr/ppermute | solution.py:30
  423.9 10.6 %collective-permute-start.2 = (f32[32,1152]{1,0:T(8,128)}, f32[32,1152]{1,0:T(8,128)S(1)}, u32[]{:S(2)}, u32[]{:S(2)}) collective-permute-start(f32[32,1152]{1,0:T(8,128)} %convolution_add_fusion.1), channel_id=1, source_target_pairs={{0,88},{8,96},{16,104},{24,112},{32,120},{40,128},{48,136},{56,144... | collective-permute-start | bytes 442376 | tf_op jit(solution)/shard_map/ppermute | solution.py:30
Sparse Core Ops, SparseCore 0:
  9.1 113.3 all-gather.4
  124.3 108.5 all-gather.6
